TPU v7x, 32 devices: a whole 2x2x4 slice. The times are simulated.
32 devices in a mesh: grp: 2 (over y), seq: 4 (over z), fsdp: 2 (over x), head: 2 (over core).
Axes of the slice: x: 2, y: 2, z: 4, core: 2. Of those that a mesh axis runs over, the one named last changes fastest.
Arguments:
- tokens: bfloat16 [6144, 3072], P(('grp', 'seq'), 'head'), parts along dimension 0
- qkv_weight: bfloat16 [3072, 1536], P('fsdp', 'head'), may hold values from -0.109375 to 0.109375
- shift_mod: float32 [6144], P('grp'), parts along dimension 0, may hold values from -3 to 3
- scale_mod: float32 [6144], P('grp'), parts along dimension 0, may hold values from -2 to 2
- q_gain: float32 [4, 128], P(('fsdp', 'head'))
- k_gain: float32 [4, 128], P(('fsdp', 'head'))
- cached: bfloat16 [6144, 512], P(('grp', 'seq'), ('fsdp', 'head')), parts along dimension 0, may hold values from -6 to 6
- active: int32 [48], P(('grp', 'seq')), parts along dimension 0, may hold values from -1 to 5, as said below
- cache_slot: int32 [48], P(('grp', 'seq')), parts along dimension 0, may hold values from 0 to 5, as said below
Outputs:
- blended: bfloat16 [6144, 512], P(('grp', 'seq'), ('fsdp', 'head')), parts along dimension 0
There are 2 independent parts, one for each index of `grp`. A program takes and returns all parts, laid end to end along the dimension named above; an argument that names none is the same for every part. Nothing has to cross between parts.
Inputs may be any that keep to these rules, and one draw needn't show every extreme that they name: Entries s * 6 to s * 6 + 5 list the active local blocks of index s of seq in rising order, each at most once, followed by -1 for the rest. Over the whole sequence exactly 12 blocks are active; some index of seq has all 6 blocks active and some has none. `cache_slot`: entries s * 6 to s * 6 + 5 are a permutation of 0 to 5.
All inputs are finite; a program needn't handle non-finite values.
Results may differ from a plain program's by a relative error of at most 0.012.
The roundings to bfloat16 on the way count: a program that leaves them out, or rounds other values in their place, can miss the bound.
Values may be sent and summed in bfloat16 or wider, within the bound.
No kernel may reach another device: no remote copies, remote signals or barrier semaphores. Data moves between devices by JAX's collectives and lax.ppermute only.
A program may use at most 64 MiB of HBM per device.

v0:
```python
import jax
import jax.numpy as jnp
from jax import lax
from jax.sharding import PartitionSpec as P

eps_norm = 1e-06


def rms_scaled(vector, gain_row):
    return (
        vector * lax.rsqrt(jnp.mean(vector * vector, axis=-1, keepdims=True) + eps_norm) * gain_row
    )


def attend_span(carry_state, queries, key_rows, value_rows):
    maxima, totals, accumulated = carry_state
    score_scale = key_rows.shape[1] ** (-0.5)
    scores = (
        jnp.einsum("qd,kd->qk", queries, key_rows, preferred_element_type=jnp.float32) * score_scale
    )
    new_max = jnp.maximum(maxima, jnp.max(scores, axis=1))
    weights = jnp.exp(scores - new_max[:, None])
    shrink = jnp.exp(maxima - new_max)
    totals = totals * shrink + jnp.sum(weights, axis=1)
    accumulated = accumulated * shrink[:, None] + jnp.dot(
        weights.astype(jnp.bfloat16), value_rows, preferred_element_type=jnp.float32
    )
    return (new_max, totals, accumulated)


def attend_keys(carry_state, queries, key_rows, value_rows):
    row_count = key_rows.shape[0]

    def block_step(block_index, journey):
        start_row = block_index * 512
        key_part = lax.dynamic_slice_in_dim(key_rows, start_row, 512, 0)
        value_part = lax.dynamic_slice_in_dim(value_rows, start_row, 512, 0)
        return attend_span(journey, queries, key_part, value_part)

    return lax.fori_loop(0, row_count // 512, block_step, carry_state)


def per_device(
    tokens, qkv_weight, shift_mod, scale_mod, q_gain, k_gain, cached, active, cache_slot
):
    gathered = lax.all_gather(tokens, "head", axis=1, tiled=True).astype(jnp.float32)
    row_mean = jnp.mean(gathered, axis=1, keepdims=True)
    centred = gathered - row_mean
    row_var = jnp.mean(centred * centred, axis=1, keepdims=True)
    normed = (centred * lax.rsqrt(row_var + eps_norm) * (1.0 + scale_mod) + shift_mod).astype(
        jnp.bfloat16
    )
    columns = lax.all_to_all(qkv_weight, "fsdp", split_axis=1, concat_axis=0, tiled=True)
    head_dim = columns.shape[1] // 3
    projected = jnp.dot(normed, columns, preferred_element_type=jnp.float32)
    queries = rms_scaled(projected[:, :head_dim], q_gain).astype(jnp.bfloat16)
    key_rows = rms_scaled(projected[:, head_dim : 2 * head_dim], k_gain).astype(jnp.bfloat16)
    values = projected[:, 2 * head_dim :].astype(jnp.bfloat16)
    tok_rows = tokens.shape[0]
    blocks = active.shape[0]
    block_rows = tok_rows // blocks
    query_blocks = queries.reshape(blocks, block_rows, head_dim)
    slot_ids = jnp.where(active >= 0, active, 0)
    chosen = jnp.take(query_blocks, slot_ids, axis=0).reshape(blocks * block_rows, head_dim)
    query_count = chosen.shape[0]
    start_state = (
        jnp.full((query_count,), -1e30, jnp.float32),
        jnp.zeros((query_count,), jnp.float32),
        jnp.zeros((query_count, head_dim), jnp.float32),
    )
    maxima, totals, accumulated = attend_keys(
        start_state,
        chosen,
        lax.all_gather(key_rows, "seq", axis=0, tiled=True),
        lax.all_gather(values, "seq", axis=0, tiled=True),
    )
    attended = (accumulated / totals[:, None]).astype(jnp.bfloat16)
    slot_rows = attended.reshape(blocks, block_rows, head_dim)
    local_ids = jnp.arange(blocks, dtype=jnp.int32)
    hit_mask = active[None, :] == local_ids[:, None]
    taken = jnp.any(hit_mask, axis=1)
    position = jnp.sum(jnp.where(hit_mask, local_ids[None, :], 0), axis=1)
    fresh_rows = jnp.take(slot_rows, position, axis=0)
    stale_rows = jnp.take(cached.reshape(blocks, block_rows, head_dim), cache_slot, axis=0)
    blended = jnp.where(taken[:, None, None], fresh_rows, stale_rows)
    return blended.reshape(tok_rows, head_dim)


def solution(mesh):
    in_specs = (
        P(("grp", "seq"), "head"),
        P("fsdp", "head"),
        P("grp"),
        P("grp"),
        P(("fsdp", "head"), None),
        P(("fsdp", "head"), None),
        P(("grp", "seq"), ("fsdp", "head")),
        P(("grp", "seq")),
        P(("grp", "seq")),
    )
    out_specs = P(("grp", "seq"), ("fsdp", "head"))
    return jax.shard_map(
        per_device, mesh=mesh, in_specs=in_specs, out_specs=out_specs, check_vma=False
    )
```

profile of v0, /device:TPU:0, one launch (start us, length us, event | category | flops | bytes accessed | tf_op | source)
XLA Modules:
  0.0 116.9 jit_solution(1242417644816890714)
XLA Ops:
  6.5 0.7 all-gather.2.cloned.1.call-update
  7.3 1.0 copy-done.2
  8.2 2.5 %copy.12 = bf16[1536,768]{0,1:T(8,128)(2,1)} copy(bf16[1536,768]{1,0:T(8,128)(2,1)S(1)} %copy-done.2) | data formatting | bytes 4718592 | tf_op args[1]
  10.8 5.1 %all-to-all-start = ((bf16[1536,2,384]{0,2,1:T(8,128)(2,1)}), bf16[1536,2,384]{0,2,1:T(8,128)(2,1)}, u32[]{:S(2)}, u32[]{:S(2)}) async-start(bf16[1536,2,384]{0,2,1:T(8,128)(2,1)} %bitcast), calls=%async_computation | async-start | bytes 4718592 | tf_op jit(solution)/shard_map/all_to_all | solution.py:53
  15.9 0.6 gather_fusion.2
  16.8 28.2 %all-to-all-done = bf16[1536,2,384]{0,2,1:T(8,128)(2,1)} async-done(((bf16[1536,2,384]{0,2,1:T(8,128)(2,1)}), bf16[1536,2,384]{0,2,1:T(8,128)(2,1)}, u32[]{:S(2)}, u32[]{:S(2)}) %all-to-all-start) | async-done | bytes 2359328 | tf_op jit(solution)/shard_map/all_to_all | solution.py:53
  45.0 3.0 %copy.13 = bf16[2,1536,384]{2,1,0:T(8,128)(2,1)S(1)} copy(bf16[2,1536,384]{1,2,0:T(8,128)(2,1)} %bitcast.1) | data formatting | bytes 4718592 | tf_op jit(solution)/shard_map/all_to_all | solution.py:53
  48.1 3.2 %convert_reduce_fusion = f32[768]{0:T(1024)S(1)} fusion(bf16[768,3072]{1,0:T(8,128)(2,1)} %all-gather.2.cloned.1.call-done), kind=kLoop, calls=%fused_computation.19 | loop fusion | flops 4717824 | bytes 4721664 | tf_op jit(solution)/shard_map/reduce_sum | solution.py:47
  51.3 0.6 copy-done.1
  51.9 1.4 %fusion.11 = f32[768]{0:T(1024)S(1)} fusion(bf16[768,3072]{1,0:T(8,128)(2,1)S(1)} %copy-done.1, f32[768]{0:T(1024)S(1)} %broadcast_multiply_fusion), kind=kLoop, calls=%fused_computation.22 | loop fusion | flops 9436416 | bytes 4724736 | tf_op jit(solution)/shard_map/reduce_sum | solution.py:49
  53.3 2.7 %fusion.15 = f32[768,384]{1,0:T(8,128)S(1)} fusion(bf16[3072,384]{1,0:T(8,128)(2,1)S(1)} %bitcast.16, bf16[768,3072]{1,0:T(8,128)(2,1)S(1)} %copy-done.1, f32[3072]{0:T(1024)S(1)} %copy-done.7, f32[3072]{0:T(1024)S(1)} %broadcast_add_fusion, f32[768]{0:T(1024)S(1)} %add_rsqrt_fusion.2, f32[768]{0:T(1024)S(1)} %broadcast_multiply_fusion), kind=kOutput, calls=%fused_computation.26 | convolution fusion | flops 1826095104 | bytes 8288256 | tf_op jit(solution)/shard_map/dot_general | solution.py:55
  56.0 0.3 multiply_reduce_fusion
  56.3 0.3 multiply_convert_fusion
  56.6 20.1 %all_gather.10 = bf16[3072,128]{1,0:T(8,128)(2,1)S(1)} all-gather(bf16[768,128]{1,0:T(8,128)(2,1)S(1)} %get-tuple-element.180), channel_id=1, replica_groups=mesh['grp'=2,'seq'=4,'fsdp'=2,'head'=2] {'seq'}, dimensions={0}, use_global_device_ids=true | all-gather | bytes 983040 | tf_op jit(solution)/shard_map/all_gather | solution.py:74
  76.7 18.1 %all_gather.11 = bf16[3072,128]{1,0:T(8,128)(2,1)} all-gather(bf16[768,128]{1,0:T(8,128)(2,1)S(1)} %slice.27), channel_id=1, replica_groups=mesh['grp'=2,'seq'=4,'fsdp'=2,'head'=2] {'seq'}, dimensions={0}, use_global_device_ids=true | all-gather | bytes 983040 | tf_op jit(solution)/shard_map/all_gather | solution.py:75
  94.8 0.6 gather_fusion
  95.5 12.9 %while.18 = (s32[]{:T(128)}, f32[768]{0:T(1024)S(1)}, f32[768]{0:T(1024)S(1)}, f32[768,128]{1,0:T(8,128)S(1)}, bf16[3072,128]{1,0:T(8,128)(2,1)S(1)}, /*index=5*...) while((s32[]{:T(128)}, f32[768]{0:T(1024)S(1)}, ...), condition=%wide.region_8.10_spmd.clone, body=%wide.region_5.9_spmd.clone.sunk | while | flops 203984640 | bytes 6013111 | solution.py:40
  95.5 0.4 fusion.34
  96.2 1.4 %convolution_add_fusion.2 = f32[768,128]{1,0:T(8,128)S(1)} fusion(f32[512,768]{1,0:T(8,128)S(1)} %get-tuple-element.233, f32[768]{0:T(1024)S(1)} %select_maximum_fusion.2, f32[768,128]{1,0:T(8,128)S(1)} %get-tuple-element.250, f32[768]{0:T(1024)S(1)} %get-tuple-element.235, pred[]{:T(512)S(6)} %compare.3, bf16[3072,128]{1,0:T(8,128)(2,1)} %get-tuple-element.264, ...), kind=kOutput, calls=%fused_computation.7.clone.1 | convolution fusion | flops 101744640 | bytes 2496517 | tf_op jit(solution)/shard_map/while/body/eval_jaxpr/dot_general | solution.py:25
  97.7 0.4 fusion.34
  98.1 0.3 fusion.35
  98.4 1.4 %convolution_add_fusion.2 = f32[768,128]{1,0:T(8,128)S(1)} fusion(f32[512,768]{1,0:T(8,128)S(1)} %get-tuple-element.233, f32[768]{0:T(1024)S(1)} %select_maximum_fusion.2, f32[768,128]{1,0:T(8,128)S(1)} %get-tuple-element.250, f32[768]{0:T(1024)S(1)} %get-tuple-element.235, pred[]{:T(512)S(6)} %compare.3, bf16[3072,128]{1,0:T(8,128)(2,1)} %get-tuple-element.264, ...), kind=kOutput, calls=%fused_computation.7.clone.1 | convolution fusion | flops 101744640 | bytes 2496517 | tf_op jit(solution)/shard_map/while/body/eval_jaxpr/dot_general | solution.py:25
  99.8 0.4 fusion.34
  100.5 1.4 %convolution_add_fusion.2 = f32[768,128]{1,0:T(8,128)S(1)} fusion(f32[512,768]{1,0:T(8,128)S(1)} %get-tuple-element.233, f32[768]{0:T(1024)S(1)} %select_maximum_fusion.2, f32[768,128]{1,0:T(8,128)S(1)} %get-tuple-element.250, f32[768]{0:T(1024)S(1)} %get-tuple-element.235, pred[]{:T(512)S(6)} %compare.3, bf16[3072,128]{1,0:T(8,128)(2,1)} %get-tuple-element.264, ...), kind=kOutput, calls=%fused_computation.7.clone.1 | convolution fusion | flops 101744640 | bytes 2496517 | tf_op jit(solution)/shard_map/while/body/eval_jaxpr/dot_general | solution.py:25
  102.0 0.4 fusion.34
  102.7 1.4 %convolution_add_fusion.2 = f32[768,128]{1,0:T(8,128)S(1)} fusion(f32[512,768]{1,0:T(8,128)S(1)} %get-tuple-element.233, f32[768]{0:T(1024)S(1)} %select_maximum_fusion.2, f32[768,128]{1,0:T(8,128)S(1)} %get-tuple-element.250, f32[768]{0:T(1024)S(1)} %get-tuple-element.235, pred[]{:T(512)S(6)} %compare.3, bf16[3072,128]{1,0:T(8,128)(2,1)} %get-tuple-element.264, ...), kind=kOutput, calls=%fused_computation.7.clone.1 | convolution fusion | flops 101744640 | bytes 2496517 | tf_op jit(solution)/shard_map/while/body/eval_jaxpr/dot_general | solution.py:25
  104.2 0.4 fusion.34
  104.8 1.4 %convolution_add_fusion.2 = f32[768,128]{1,0:T(8,128)S(1)} fusion(f32[512,768]{1,0:T(8,128)S(1)} %get-tuple-element.233, f32[768]{0:T(1024)S(1)} %select_maximum_fusion.2, f32[768,128]{1,0:T(8,128)S(1)} %get-tuple-element.250, f32[768]{0:T(1024)S(1)} %get-tuple-element.235, pred[]{:T(512)S(6)} %compare.3, bf16[3072,128]{1,0:T(8,128)(2,1)} %get-tuple-element.264, ...), kind=kOutput, calls=%fused_computation.7.clone.1 | convolution fusion | flops 101744640 | bytes 2496517 | tf_op jit(solution)/shard_map/while/body/eval_jaxpr/dot_general | solution.py:25
  106.3 0.4 fusion.34
  107.0 1.4 %convolution_add_fusion.2 = f32[768,128]{1,0:T(8,128)S(1)} fusion(f32[512,768]{1,0:T(8,128)S(1)} %get-tuple-element.233, f32[768]{0:T(1024)S(1)} %select_maximum_fusion.2, f32[768,128]{1,0:T(8,128)S(1)} %get-tuple-element.250, f32[768]{0:T(1024)S(1)} %get-tuple-element.235, pred[]{:T(512)S(6)} %compare.3, bf16[3072,128]{1,0:T(8,128)(2,1)} %get-tuple-element.264, ...), kind=kOutput, calls=%fused_computation.7.clone.1 | convolution fusion | flops 101744640 | bytes 2496517 | tf_op jit(solution)/shard_map/while/body/eval_jaxpr/dot_general | solution.py:25
  108.6 0.6 gather_fusion.1
  109.2 0.8 select_select_fusion
  (60 shorter events, 2.1 us)
Async XLA Ops:
  6.5 9.4 %copy-start = (bf16[768,128]{1,0:T(8,128)(2,1)S(1)}, bf16[768,128]{1,0:T(8,128)(2,1)}, u32[]{:S(2)}) copy-start(bf16[768,128]{1,0:T(8,128)(2,1)} %param.19) | copy-start | bytes 589828
  6.5 1.7 %copy-start.2 = (bf16[1536,768]{1,0:T(8,128)(2,1)S(1)}, bf16[1536,768]{1,0:T(8,128)(2,1)}, u32[]{:S(2)}) copy-start(bf16[1536,768]{1,0:T(8,128)(2,1)} %param.14) | copy-start | bytes 7077892
  6.5 41.5 %all-gather.2.cloned.1.call-start = ((), (), s32[]{:S(2)}) async-start(), calls=%async_computation.1 | async-start | bytes 7077888 | tf_op jit(solution)/shard_map/all_gather | solution.py:46
  10.8 5.1 %copy-start.6 = (s32[6]{0:T(128)S(1)}, s32[6]{0:T(128)}, u32[]{:S(2)}) copy-start(s32[6]{0:T(128)} %param.21) | copy-start | bytes 76
  10.8 5.8 %copy-start.8 = (s32[6]{0:T(128)S(1)}, s32[6]{0:T(128)}, u32[]{:S(2)}) copy-start(s32[6]{0:T(128)} %param.20) | copy-start | bytes 76
  10.8 6.1 %copy-start.3 = (f32[3072]{0:T(1024)S(1)}, f32[3072]{0:T(1024)}, u32[]{:S(2)}) copy-start(f32[3072]{0:T(1024)} %param.16) | copy-start | bytes 36868
  10.8 34.3 %all-to-all-start = ((bf16[1536,2,384]{0,2,1:T(8,128)(2,1)}), bf16[1536,2,384]{0,2,1:T(8,128)(2,1)}, u32[]{:S(2)}, u32[]{:S(2)}) async-start(bf16[1536,2,384]{0,2,1:T(8,128)(2,1)} %bitcast), calls=%async_computation | async-start | bytes 4718592 | tf_op jit(solution)/shard_map/all_to_all | solution.py:53
  48.1 3.8 %copy-start.1 = (bf16[768,3072]{1,0:T(8,128)(2,1)S(1)}, bf16[768,3072]{1,0:T(8,128)(2,1)}, u32[]{:S(2)}) copy-start(bf16[768,3072]{1,0:T(8,128)(2,1)} %all-gather.2.cloned.1.call-done) | copy-start | bytes 14155780
  51.9 1.4 %copy-start.7 = (f32[3072]{0:T(1024)S(1)}, f32[3072]{0:T(1024)}, u32[]{:S(2)}) copy-start(f32[3072]{0:T(1024)} %param.15) | copy-start | bytes 36868
  53.2 3.1 %copy-start.4 = (f32[1,128]{1,0:T(1,128)S(1)}, f32[1,128]{1,0:T(1,128)}, u32[]{:S(2)}) copy-start(f32[1,128]{1,0:T(1,128)} %param.17) | copy-start | bytes 1540
  53.2 3.1 %copy-start.5 = (f32[1,128]{1,0:T(1,128)S(1)}, f32[1,128]{1,0:T(1,128)}, u32[]{:S(2)}) copy-start(f32[1,128]{1,0:T(1,128)} %param.18) | copy-start | bytes 1540
Sparse Core Ops, SparseCore 0:
  8.9 17.1 all-gather.1
where the time goes:
time: 117 us
  blocking collectives  38.2 us (33%)
  waiting for transfers between devices  28.9 us (25%)
  matrix products  13.7 us (12%)
  between operations  13.6 us (12%)
  local copies, waits for them, and re-layouts  8.9 us (8%)
  other arithmetic  8.08 us (7%)
  starting transfers between devices  5.07 us (4%)
    all_to_all x1, waiting for transfers between devices, per_device(): lax.all_to_all(qkv_weight, 'fsdp', split_axis=1, concat_axis=0, tiled=True)  28.2 us
    all_gather x1, blocking collectives, per_device(): lax.all_gather(key_rows, 'seq', axis=0, tiled=True)  20.1 us
    all_gather x1, blocking collectives, per_device(): lax.all_gather(values, 'seq', axis=0, tiled=True)  18.1 us
    dot_general x6, matrix products, attend_span(): jnp.dot(weights.astype(jnp.bfloat16), value_rows, preferred_element_type=...  8.68 us
    all_to_all x1, starting transfers between devices, per_device(): lax.all_to_all(qkv_weight, 'fsdp', split_axis=1, concat_axis=0, tiled=True)  5.07 us
    unnamed x19, local copies, waits for them, and re-layouts  4.09 us
    reduce_sum x1, other arithmetic, per_device(): row_mean = jnp.mean(gathered, axis=1, keepdims=True)  3.17 us
    all_to_all x1, local copies, waits for them, and re-layouts, per_device(): lax.all_to_all(qkv_weight, 'fsdp', split_axis=1, concat_axis=0, tiled=True)  3.02 us
  transfers between devices with their start and end apart: 2, of which 1 were waited for; matrix products, arithmetic and copies ran while one was open for 5% of the time, Pallas kernels for 0%

commit v1 on v0

--- a/solution.py
+++ b/solution.py
@@ -4,6 +4,12 @@
 from jax.sharding import PartitionSpec as P
 
 eps_norm = 1e-06
+
+
+def swap_blocks(x, axis, split, join):
+    parts = jnp.split(x, lax.axis_size(axis), axis=split)
+    arrived = lax.all_to_all(jnp.stack(parts), axis, 0, 0)
+    return jnp.concatenate(arrived, axis=join)
 
 
 def rms_scaled(vector, gain_row):
@@ -50,7 +56,7 @@
     normed = (centred * lax.rsqrt(row_var + eps_norm) * (1.0 + scale_mod) + shift_mod).astype(
         jnp.bfloat16
     )
-    columns = lax.all_to_all(qkv_weight, "fsdp", split_axis=1, concat_axis=0, tiled=True)
+    columns = swap_blocks(qkv_weight, "fsdp", 1, 0)
     head_dim = columns.shape[1] // 3
     projected = jnp.dot(normed, columns, preferred_element_type=jnp.float32)
     queries = rms_scaled(projected[:, :head_dim], q_gain).astype(jnp.bfloat16)

time: 117 us -> 109 us (0.932)
  waiting for transfers between devices: 28.9 us -> 23.3 us
  local copies, waits for them, and re-layouts: 8.9 us -> 3.61 us
  matrix products: 13.7 us -> 15.7 us
  other arithmetic: 8.08 us -> 9.79 us
    all_to_all x1, waiting for transfers between devices: 28.2 us -> 12.1 us  [swap_blocks(): arrived = lax.all_to_all(jnp.stack(parts), axis, 0, 0)]
    all_gather x1, waiting for transfers between devices: 0.02 us -> 10.6 us  [per_device(): lax.all_gather(tokens, 'head', axis=1, tiled=True).astype(jnp.float32)]
    all_to_all x1 -> x0, local copies, waits for them, and re-layouts: 3.02 us -> none  [per_device(): lax.all_to_all(qkv_weight, 'fsdp', split_axis=1, concat_axis=0, tiled=True)]
    unnamed x19 -> x18, local copies, waits for them, and re-layouts: 4.09 us -> 1.58 us
    dot_general x1, matrix products: 2.73 us -> 4.76 us  [per_device(): projected = jnp.dot(normed, columns, preferred_element_type=jnp.float32)]
    another operation x0 -> x1, other arithmetic: none -> 1.71 us  [swap_blocks(): arrived = lax.all_to_all(jnp.stack(parts), axis, 0, 0)]
  transfers between devices with their start and end apart: 2 -> 2, of which waited for: 1 -> 2; matrix products, arithmetic and copies ran while one was open for 5% -> 7% of each run, Pallas kernels for 0% -> 0%
where the time goes in v1:
time: 109 us
  blocking collectives  38.2 us (35%)
  waiting for transfers between devices  23.3 us (21%)
  matrix products  15.7 us (14%)
  between operations  13.6 us (12%)
  other arithmetic  9.79 us (9%)
  starting transfers between devices  4.37 us (4%)
  local copies, waits for them, and re-layouts  3.61 us (3%)
    all_gather x1, blocking collectives, per_device(): lax.all_gather(key_rows, 'seq', axis=0, tiled=True)  20.1 us
    all_gather x1, blocking collectives, per_device(): lax.all_gather(values, 'seq', axis=0, tiled=True)  18.1 us
    all_to_all x1, waiting for transfers between devices, swap_blocks(): arrived = lax.all_to_all(jnp.stack(parts), axis, 0, 0)  12.1 us
    all_gather x1, waiting for transfers between devices, per_device(): lax.all_gather(tokens, 'head', axis=1, tiled=True).astype(jnp.float32)  10.6 us
    dot_general x6, matrix products, attend_span(): jnp.dot(weights.astype(jnp.bfloat16), value_rows, preferred_element_type=...  8.68 us
    dot_general x1, matrix products, per_device(): projected = jnp.dot(normed, columns, preferred_element_type=jnp.float32)  4.76 us
    all_to_all x1, starting transfers between devices, swap_blocks(): arrived = lax.all_to_all(jnp.stack(parts), axis, 0, 0)  4.37 us
    reduce_sum x1, other arithmetic, per_device(): row_mean = jnp.mean(gathered, axis=1, keepdims=True)  3.17 us
  transfers between devices with their start and end apart: 2, of which 2 were waited for; matrix products, arithmetic and copies ran while one was open for 7% of the time, Pallas kernels for 0%

profile of v1, /device:TPU:0, one launch (start us, length us, event | category | flops | bytes accessed | tf_op | source)
XLA Modules:
  0.0 108.9 jit_solution(11883256424376087553)
XLA Ops:
  6.5 0.7 all-gather.2.cloned.1.call-update
  7.3 1.0 copy-done.2
  8.5 1.7 %pad_maximum_fusion = bf16[2,1536,384]{2,1,0:T(8,128)(2,1)} fusion(bf16[1,1536,384]{2,1,0:T(8,128)(2,1)S(1)} %get-tuple-element.180, bf16[1,1536,384]{2,1,0:T(8,128)(2,1)S(1)} %get-tuple-element.179), kind=kLoop, calls=%fused_computation.31 | loop fusion | flops 1179648 | bytes 4718592 | tf_op jit(solution)/shard_map/stack | solution.py:11
  10.2 4.4 %all-to-all-start = ((bf16[2,1536,384]{2,1,0:T(8,128)(2,1)}), bf16[2,1536,384]{2,1,0:T(8,128)(2,1)S(1)}, u32[]{:S(2)}, u32[]{:S(2)}) async-start(bf16[2,1536,384]{2,1,0:T(8,128)(2,1)} %pad_maximum_fusion), calls=%async_computation | async-start | bytes 4718592 | tf_op jit(solution)/shard_map/all_to_all | solution.py:11
  14.6 0.6 gather_fusion.2
  15.5 10.6 %all-gather.2.cloned.1.call-done = bf16[768,3072]{1,0:T(8,128)(2,1)} async-done(((bf16[768,1536]{1,0:T(8,128)(2,1)}), bf16[768,3072]{1,0:T(8,128)(2,1)}) %all-gather.2.cloned.1.call-update) | async-done | bytes 4718608 | tf_op jit(solution)/shard_map/all_gather | solution.py:52
  26.1 3.2 %convert_reduce_fusion = f32[768]{0:T(1024)S(1)} fusion(bf16[768,3072]{1,0:T(8,128)(2,1)} %all-gather.2.cloned.1.call-done), kind=kLoop, calls=%fused_computation.19 | loop fusion | flops 4717824 | bytes 4721664 | tf_op jit(solution)/shard_map/reduce_sum | solution.py:53
  29.3 0.6 copy-done.1
  29.8 1.4 %fusion.11 = f32[768]{0:T(1024)S(1)} fusion(bf16[768,3072]{1,0:T(8,128)(2,1)S(1)} %copy-done.1, f32[768]{0:T(1024)S(1)} %broadcast_multiply_fusion), kind=kLoop, calls=%fused_computation.22 | loop fusion | flops 9436416 | bytes 4724736 | tf_op jit(solution)/shard_map/reduce_sum | solution.py:55
  31.2 12.1 %all-to-all-done = bf16[2,1536,384]{2,1,0:T(8,128)(2,1)S(1)} async-done(((bf16[2,1536,384]{2,1,0:T(8,128)(2,1)}), bf16[2,1536,384]{2,1,0:T(8,128)(2,1)S(1)}, u32[]{:S(2)}, u32[]{:S(2)}) %all-to-all-start) | async-done | bytes 2359328 | tf_op jit(solution)/shard_map/all_to_all | solution.py:11
  43.3 4.8 %fusion.15 = f32[768,384]{1,0:T(8,128)S(1)} fusion(bf16[3072,384]{1,0:T(8,128)(2,1)S(1)} %bitcast.18, bf16[768,3072]{1,0:T(8,128)(2,1)} %all-gather.2.cloned.1.call-done, f32[3072]{0:T(1024)S(1)} %copy-done.7, f32[3072]{0:T(1024)S(1)} %broadcast_add_fusion, f32[768]{0:T(1024)S(1)} %add_rsqrt_fusion.2, f32[768]{0:T(1024)S(1)} %broadcast_multiply_fusion), kind=kOutput, calls=%fused_computation.26 | convolution fusion | flops 1826095104 | bytes 8288256 | tf_op jit(solution)/shard_map/dot_general | solution.py:61
  48.1 0.3 multiply_reduce_fusion
  48.4 0.3 multiply_convert_fusion
  48.7 20.1 %all_gather.10 = bf16[3072,128]{1,0:T(8,128)(2,1)S(1)} all-gather(bf16[768,128]{1,0:T(8,128)(2,1)S(1)} %get-tuple-element.182), channel_id=1, replica_groups=mesh['grp'=2,'seq'=4,'fsdp'=2,'head'=2] {'seq'}, dimensions={0}, use_global_device_ids=true | all-gather | bytes 983040 | tf_op jit(solution)/shard_map/all_gather | solution.py:80
  68.8 18.1 %all_gather.11 = bf16[3072,128]{1,0:T(8,128)(2,1)} all-gather(bf16[768,128]{1,0:T(8,128)(2,1)S(1)} %slice.27), channel_id=1, replica_groups=mesh['grp'=2,'seq'=4,'fsdp'=2,'head'=2] {'seq'}, dimensions={0}, use_global_device_ids=true | all-gather | bytes 983040 | tf_op jit(solution)/shard_map/all_gather | solution.py:81
  86.9 0.6 gather_fusion
  87.6 12.9 %while.18 = (s32[]{:T(128)}, f32[768]{0:T(1024)S(1)}, f32[768]{0:T(1024)S(1)}, f32[768,128]{1,0:T(8,128)S(1)}, bf16[3072,128]{1,0:T(8,128)(2,1)S(1)}, /*index=5*...) while((s32[]{:T(128)}, f32[768]{0:T(1024)S(1)}, ...), condition=%wide.region_8.10_spmd.clone, body=%wide.region_5.9_spmd.clone.sunk | while | flops 203984640 | bytes 6013111 | solution.py:46
  87.6 0.4 fusion.34
  88.0 0.3 fusion.35
  88.3 1.4 %convolution_add_fusion.2 = f32[768,128]{1,0:T(8,128)S(1)} fusion(f32[512,768]{1,0:T(8,128)S(1)} %get-tuple-element.235, f32[768]{0:T(1024)S(1)} %select_maximum_fusion.2, f32[768,128]{1,0:T(8,128)S(1)} %get-tuple-element.252, f32[768]{0:T(1024)S(1)} %get-tuple-element.237, pred[]{:T(512)S(6)} %compare.3, bf16[3072,128]{1,0:T(8,128)(2,1)} %get-tuple-element.266, ...), kind=kOutput, calls=%fused_computation.7.clone.1 | convolution fusion | flops 101744640 | bytes 2496517 | tf_op jit(solution)/shard_map/while/body/eval_jaxpr/dot_general | solution.py:31
  89.7 0.4 fusion.34
  90.4 1.4 %convolution_add_fusion.2 = f32[768,128]{1,0:T(8,128)S(1)} fusion(f32[512,768]{1,0:T(8,128)S(1)} %get-tuple-element.235, f32[768]{0:T(1024)S(1)} %select_maximum_fusion.2, f32[768,128]{1,0:T(8,128)S(1)} %get-tuple-element.252, f32[768]{0:T(1024)S(1)} %get-tuple-element.237, pred[]{:T(512)S(6)} %compare.3, bf16[3072,128]{1,0:T(8,128)(2,1)} %get-tuple-element.266, ...), kind=kOutput, calls=%fused_computation.7.clone.1 | convolution fusion | flops 101744640 | bytes 2496517 | tf_op jit(solution)/shard_map/while/body/eval_jaxpr/dot_general | solution.py:31
  91.9 0.4 fusion.34
  92.6 1.4 %convolution_add_fusion.2 = f32[768,128]{1,0:T(8,128)S(1)} fusion(f32[512,768]{1,0:T(8,128)S(1)} %get-tuple-element.235, f32[768]{0:T(1024)S(1)} %select_maximum_fusion.2, f32[768,128]{1,0:T(8,128)S(1)} %get-tuple-element.252, f32[768]{0:T(1024)S(1)} %get-tuple-element.237, pred[]{:T(512)S(6)} %compare.3, bf16[3072,128]{1,0:T(8,128)(2,1)} %get-tuple-element.266, ...), kind=kOutput, calls=%fused_computation.7.clone.1 | convolution fusion | flops 101744640 | bytes 2496517 | tf_op jit(solution)/shard_map/while/body/eval_jaxpr/dot_general | solution.py:31
  94.0 0.4 fusion.34
  94.7 1.4 %convolution_add_fusion.2 = f32[768,128]{1,0:T(8,128)S(1)} fusion(f32[512,768]{1,0:T(8,128)S(1)} %get-tuple-element.235, f32[768]{0:T(1024)S(1)} %select_maximum_fusion.2, f32[768,128]{1,0:T(8,128)S(1)} %get-tuple-element.252, f32[768]{0:T(1024)S(1)} %get-tuple-element.237, pred[]{:T(512)S(6)} %compare.3, bf16[3072,128]{1,0:T(8,128)(2,1)} %get-tuple-element.266, ...), kind=kOutput, calls=%fused_computation.7.clone.1 | convolution fusion | flops 101744640 | bytes 2496517 | tf_op jit(solution)/shard_map/while/body/eval_jaxpr/dot_general | solution.py:31
  96.2 0.4 fusion.34
  96.9 1.4 %convolution_add_fusion.2 = f32[768,128]{1,0:T(8,128)S(1)} fusion(f32[512,768]{1,0:T(8,128)S(1)} %get-tuple-element.235, f32[768]{0:T(1024)S(1)} %select_maximum_fusion.2, f32[768,128]{1,0:T(8,128)S(1)} %get-tuple-element.252, f32[768]{0:T(1024)S(1)} %get-tuple-element.237, pred[]{:T(512)S(6)} %compare.3, bf16[3072,128]{1,0:T(8,128)(2,1)} %get-tuple-element.266, ...), kind=kOutput, calls=%fused_computation.7.clone.1 | convolution fusion | flops 101744640 | bytes 2496517 | tf_op jit(solution)/shard_map/while/body/eval_jaxpr/dot_general | solution.py:31
  98.4 0.4 fusion.34
  99.0 1.4 %convolution_add_fusion.2 = f32[768,128]{1,0:T(8,128)S(1)} fusion(f32[512,768]{1,0:T(8,128)S(1)} %get-tuple-element.235, f32[768]{0:T(1024)S(1)} %select_maximum_fusion.2, f32[768,128]{1,0:T(8,128)S(1)} %get-tuple-element.252, f32[768]{0:T(1024)S(1)} %get-tuple-element.237, pred[]{:T(512)S(6)} %compare.3, bf16[3072,128]{1,0:T(8,128)(2,1)} %get-tuple-element.266, ...), kind=kOutput, calls=%fused_computation.7.clone.1 | convolution fusion | flops 101744640 | bytes 2496517 | tf_op jit(solution)/shard_map/while/body/eval_jaxpr/dot_general | solution.py:31
  100.7 0.6 gather_fusion.1
  101.3 0.8 select_select_fusion
  (60 shorter events, 2.3 us)
Async XLA Ops:
  6.5 8.1 %copy-start = (bf16[768,128]{1,0:T(8,128)(2,1)S(1)}, bf16[768,128]{1,0:T(8,128)(2,1)}, u32[]{:S(2)}) copy-start(bf16[768,128]{1,0:T(8,128)(2,1)} %param.19) | copy-start | bytes 589828
  6.5 1.7 %copy-start.2 = (bf16[1536,768]{1,0:T(8,128)(2,1)S(1)}, bf16[1536,768]{1,0:T(8,128)(2,1)}, u32[]{:S(2)}) copy-start(bf16[1536,768]{1,0:T(8,128)(2,1)} %param.14) | copy-start | bytes 7077892
  6.5 19.5 %all-gather.2.cloned.1.call-start = ((), (), s32[]{:S(2)}) async-start(), calls=%async_computation.1 | async-start | bytes 7077888 | tf_op jit(solution)/shard_map/all_gather | solution.py:52
  10.2 4.4 %copy-start.6 = (s32[6]{0:T(128)S(1)}, s32[6]{0:T(128)}, u32[]{:S(2)}) copy-start(s32[6]{0:T(128)} %param.21) | copy-start | bytes 76
  10.2 5.0 %copy-start.8 = (s32[6]{0:T(128)S(1)}, s32[6]{0:T(128)}, u32[]{:S(2)}) copy-start(s32[6]{0:T(128)} %param.20) | copy-start | bytes 76
  10.2 5.3 %copy-start.3 = (f32[3072]{0:T(1024)S(1)}, f32[3072]{0:T(1024)}, u32[]{:S(2)}) copy-start(f32[3072]{0:T(1024)} %param.16) | copy-start | bytes 36868
  10.2 33.1 %all-to-all-start = ((bf16[2,1536,384]{2,1,0:T(8,128)(2,1)}), bf16[2,1536,384]{2,1,0:T(8,128)(2,1)S(1)}, u32[]{:S(2)}, u32[]{:S(2)}) async-start(bf16[2,1536,384]{2,1,0:T(8,128)(2,1)} %pad_maximum_fusion), calls=%async_computation | async-start | bytes 4718592 | tf_op jit(solution)/shard_map/all_to_all | solution.py:11
  26.1 3.8 %copy-start.1 = (bf16[768,3072]{1,0:T(8,128)(2,1)S(1)}, bf16[768,3072]{1,0:T(8,128)(2,1)}, u32[]{:S(2)}) copy-start(bf16[768,3072]{1,0:T(8,128)(2,1)} %all-gather.2.cloned.1.call-done) | copy-start | bytes 14155780
  29.8 13.4 %copy-start.7 = (f32[3072]{0:T(1024)S(1)}, f32[3072]{0:T(1024)}, u32[]{:S(2)}) copy-start(f32[3072]{0:T(1024)} %param.15) | copy-start | bytes 36868
  43.3 5.1 %copy-start.4 = (f32[1,128]{1,0:T(1,128)S(1)}, f32[1,128]{1,0:T(1,128)}, u32[]{:S(2)}) copy-start(f32[1,128]{1,0:T(1,128)} %param.17) | copy-start | bytes 1540
  43.3 5.1 %copy-start.5 = (f32[1,128]{1,0:T(1,128)S(1)}, f32[1,128]{1,0:T(1,128)}, u32[]{:S(2)}) copy-start(f32[1,128]{1,0:T(1,128)} %param.18) | copy-start | bytes 1540
Sparse Core Ops, SparseCore 0:
  8.9 17.1 all-gather.1
